TPU v7x, 32 devices: a whole 2x2x4 slice. The times are simulated.
32 devices in a mesh: cfg: 2 (over x), space: 8 (over z, y), diag: 2 (over core).
Axes of the slice: x: 2, y: 2, z: 4, core: 2. Of those that a mesh axis runs over, the one named last changes fastest.
Arguments:
- eigvecs: bfloat16 [8, 2, 3, 128, 16, 256], P('cfg', None, None, None, ('space', 'diag')), parts along dimension 0, may hold values from -6 to 6
- gauge_links: float32 [8, 3, 2, 3, 3, 16, 256], P('cfg', None, None, None, None, ('space', 'diag')), parts along dimension 0, may hold values from -6 to 6
- momenta: int32 [4, 3], replicated, may hold values from -2 to 2
- spin_mix: float32 [16, 4, 4], replicated, may hold values from -4 to 4
- perambulators: bfloat16 [64, 4, 2, 128, 512], P(('cfg', 'space', 'diag')), parts along dimension 0, may hold values from -0.375 to 0.375
- contraction_list: int32 [32, 3], P(('space', 'diag')), may hold values from 0 to 63, as said below
Outputs:
- diagrams: bfloat16 [64, 4, 2, 128, 512], P(('cfg', 'space', 'diag')), parts along dimension 0
There are 2 independent parts, one for each index of `cfg`. A program takes and returns all parts, laid end to end along the dimension named above; an argument that names none is the same for every part. Nothing has to cross between parts.
Inputs may be any that keep to these rules, and one draw needn't show every extreme that they name: `contraction_list`: row j is one diagram. Column 0 is an elemental item below 64, column 1 a spin structure below 16, column 2 a perambulator q with q // 2 == j // 2; each aligned group of 2 rows names each of its 2 perambulators exactly once.
All inputs are finite; a program needn't handle non-finite values.
Results may differ from a plain program's by a relative error of at most 0.0064.
Values may be sent and summed in bfloat16 or wider, within the bound.
A program may use at most 128 MiB of HBM per device.

v0:
```python
import functools
import math

import jax
import jax.numpy as jnp
from jax import lax
from jax.experimental import pallas as pl
from jax.experimental.pallas import tpu as pltpu
from jax.sharding import PartitionSpec as P

LX = 16
LY = 16
NDISP = 4
CHUNK = 16
MESH = pl.DeviceIdType.MESH
NT = (((1,), (1,)), ((), ()))
f32 = jnp.float32
bf16 = jnp.bfloat16


def elemental_kernel(
    dims, list_ref, alpha_ref, cos_ref, sin_ref, link_ref, eig_ref, out_ref,
    above, fields, lists, table, part1, recv1, part2, recv2, part3, recv3, own,
    v_send, v_recv, l_send, l_recv, l_local, s1, r1, s2, r2, s3, r3,
):
    nspace, ndiag, inner, local, slices, nvec, plane, factor = dims
    ndev = nspace * ndiag
    outer = nspace // inner
    space = lax.axis_index("space")
    core = lax.axis_index("diag")
    cfg = lax.axis_index("cfg")
    me = space * ndiag + core
    zpos = space // inner
    ypos = lax.rem(space, inner)

    def device(index):
        return (cfg, index // ndiag, lax.rem(index, ndiag))

    barrier = pltpu.get_barrier_semaphore()

    @pl.loop(1, ndev)
    def _(k):
        pl.semaphore_signal(
            barrier, inc=1, device_id=device(lax.rem(me + k, ndev)), device_id_type=MESH
        )

    pl.semaphore_wait(barrier, ndev - 1)

    def v_copy(t):
        return pltpu.make_async_remote_copy(
            src_ref=eig_ref.at[t], dst_ref=above.at[t],
            send_sem=v_send.at[t], recv_sem=v_recv.at[t],
            device_id=device(lax.rem(me + ndev - 1, ndev)), device_id_type=MESH,
        )

    def l_copy(k):
        return pltpu.make_async_remote_copy(
            src_ref=list_ref, dst_ref=lists.at[k],
            send_sem=l_send.at[k], recv_sem=l_recv.at[k],
            device_id=device(lax.rem(me + k, ndev)), device_id_type=MESH,
        )

    @pl.loop(1, ndev)
    def _(k):
        l_copy(k).start()

    for t in range(slices):
        v_copy(t).start()
    lists[0] = list_ref[...]

    lane = lax.broadcasted_iota(jnp.int32, (CHUNK, plane), 1)
    edge = lax.rem(lane, LX) == LX - 1

    def displace(t, direction, source):
        @pl.loop(0, nvec // CHUNK)
        def _(i):
            rows = pl.multiple_of(i * CHUNK, CHUNK)
            vec = []
            for p in range(2):
                line = []
                for c in range(3):
                    v = source[t, p, c, pl.ds(rows, CHUNK), :].astype(f32)
                    if direction == 0:
                        v = jnp.where(
                            edge, pltpu.roll(v, LX - 1, 1), pltpu.roll(v, plane - 1, 1)
                        )
                    elif direction == 1:
                        v = pltpu.roll(v, plane - LX, 1)
                    line.append(v)
                vec.append(line)
            for row in range(3):
                real = imag = None
                for col in range(3):
                    mr = link_ref[t, direction, 0, row, pl.ds(col, 1), :]
                    mi = link_ref[t, direction, 1, row, pl.ds(col, 1), :]
                    re = mr * vec[0][col] - mi * vec[1][col]
                    im = mr * vec[1][col] + mi * vec[0][col]
                    real = re if real is None else real + re
                    imag = im if imag is None else imag + im
                lanes = slice(row * plane, (row + 1) * plane)
                fields[t * NDISP + direction + 1, pl.ds(rows, CHUNK), lanes] = real.astype(bf16)
                fields[
                    t * NDISP + direction + 1, pl.ds(nvec + rows, CHUNK), lanes
                ] = imag.astype(bf16)

    @pl.loop(0, slices)
    def _(t):
        for p in range(2):
            for c in range(3):
                fields[
                    t * NDISP, p * nvec:(p + 1) * nvec, c * plane:(c + 1) * plane
                ] = eig_ref[t, p, c]
        displace(t, 0, eig_ref)
        displace(t, 1, eig_ref)

    @pl.loop(1, ndev)
    def _(k):
        l_copy(k).wait()

    to_smem = pltpu.make_async_copy(lists, table, l_local)
    to_smem.start()
    to_smem.wait()

    @pl.loop(0, slices)
    def _(t):
        v_copy(t).wait()
        displace(t, 2, above)

    def item(dest, i):
        slot = lax.rem(me + ndev - dest, ndev)
        tv = table[slot, 0, 4 * i]
        tx = table[slot, 0, 4 * i + 1]
        m = table[slot, 0, 4 * i + 2]
        md = table[slot, 0, 4 * i + 3]
        ar = alpha_ref[2 * md]
        ai = alpha_ref[2 * md + 1]
        cosine = cos_ref[pl.ds(m, 1), :]
        sine = sin_ref[pl.ds(m, 1), :]
        first = second = None
        for c in range(3):
            lanes = slice(c * plane, (c + 1) * plane)
            v = fields[tv, :, lanes]
            x = fields[tx, :, lanes].astype(f32)
            xr, xi = x[:nvec], x[nvec:]
            a, b = cosine * xr, sine * xi
            g, h = cosine * xi, sine * xr
            y = jnp.concatenate([(a + b).astype(bf16), (g - h).astype(bf16)], 0)
            z = jnp.concatenate([(a - b).astype(bf16), (g + h).astype(bf16)], 0)
            d1 = lax.dot_general(v, y, NT, preferred_element_type=f32)
            d2 = lax.dot_general(z, v, NT, preferred_element_type=f32)
            first = d1 if first is None else first + d1
            second = d2 if second is None else second + d2
        g1r = first[:nvec, :nvec] + first[nvec:, nvec:]
        g1i = first[:nvec, nvec:] - first[nvec:, :nvec]
        g2r = second[:nvec, :nvec] + second[nvec:, nvec:]
        g2i = second[:nvec, nvec:] - second[nvec:, :nvec]
        return (
            (g1r - (ar * g2r - ai * g2i)) * factor,
            (g1i - (ar * g2i + ai * g2r)) * factor,
        )

    def copy1(j):
        return pltpu.make_async_remote_copy(
            src_ref=part1.at[j], dst_ref=recv1.at[j], send_sem=s1.at[j], recv_sem=r1.at[j],
            device_id=(cfg, space, 1 - core), device_id_type=MESH,
        )

    def copy2(j):
        return pltpu.make_async_remote_copy(
            src_ref=part2.at[j], dst_ref=recv2.at[j], send_sem=s2.at[j], recv_sem=r2.at[j],
            device_id=(cfg, zpos * inner + (1 - ypos), core), device_id_type=MESH,
        )

    def copy3(j):
        return pltpu.make_async_remote_copy(
            src_ref=part3.at[j], dst_ref=recv3.at[j], send_sem=s3.at[j], recv_sem=r3.at[j],
            device_id=(cfg, lax.rem(zpos + 1 + j, outer) * inner + ypos, core),
            device_id_type=MESH,
        )

    def chip_sum(j, yway):
        zway = lax.rem(zpos + 1 + lax.rem(j, outer), outer)
        chip = (zway * inner + yway) * ndiag

        @pl.loop(0, local)
        def _(i):
            real, imag = item(chip + (1 - core), i)
            part1[j, i, 0] = real.astype(bf16)
            part1[j, i, 1] = imag.astype(bf16)

        copy1(j).start()

        @pl.loop(0, local)
        def _(i):
            real, imag = item(chip + core, i)
            own[i, 0] = real
            own[i, 1] = imag

        copy1(j).wait()

    @pl.loop(0, outer)
    def _(j):
        chip_sum(j, 1 - ypos)
        part2[j] = (own[...] + recv1[j].astype(f32)).astype(bf16)
        copy2(j).start()

    @pl.loop(0, outer)
    def _(j):
        chip_sum(j + outer, ypos)
        copy2(j).wait()
        own[...] = own[...] + recv1[j + outer].astype(f32) + recv2[j].astype(f32)

        @pl.when(j < outer - 1)
        def _():
            part3[j] = own[...].astype(bf16)
            copy3(j).start()

    @pl.loop(0, outer - 1)
    def _(j):
        copy3(j).wait()
        own[...] = own[...] + recv3[j].astype(f32)

    out_ref[...] = own[...].astype(bf16)


def diagram_kernel(pick_ref, spin_ref, elem_ref, tau_ref, out_ref):
    d = pl.program_id(0)
    g = pick_ref[d, 1]
    spins = tau_ref.shape[1]
    er, ei = elem_ref[0, 0], elem_ref[0, 1]
    square = jnp.concatenate(
        [jnp.concatenate([er, -ei], 1), jnp.concatenate([ei, er], 1)], 0
    )
    width = tau_ref.shape[3]
    step = 256 if width % 256 == 0 else width
    for start in range(0, width, step):
        blocks = [
            jnp.dot(square, tau_ref[0, s, :, start:start + step], preferred_element_type=f32)
            for s in range(spins)
        ]
        for r in range(spins):
            mixed = spin_ref[g, r * spins] * blocks[0]
            for s in range(1, spins):
                mixed = mixed + spin_ref[g, r * spins + s] * blocks[s]
            out_ref[0, r, :, start:start + step] = mixed.astype(bf16)


def body(eigvecs, gauge_links, momenta, spin_mix, perambulators, contraction_list):
    slices, _, colors, nvec, depth, plane = eigvecs.shape
    assert depth == 1 and colors == 3
    nspace, ndiag = lax.axis_size("space"), lax.axis_size("diag")
    assert ndiag == 2 and nspace % 2 == 0
    inner = 2
    outer = nspace // inner
    ndev = nspace * ndiag
    position = lax.axis_index(("space", "diag"))
    total_z = ndev
    nmom = momenta.shape[0]
    scale = 1.0 / math.sqrt(3 * plane * total_z)
    flat = jnp.arange(plane)
    moment = momenta.astype(f32)
    angle = 2.0 * math.pi * (
        moment[:, 0, None] * (flat % LX).astype(f32)[None] / LX
        + moment[:, 1, None] * (flat // LX).astype(f32)[None] / LY
        + moment[:, 2, None] * position.astype(f32) / total_z
    )
    cosine, sine = jnp.cos(angle), jnp.sin(angle)
    hop = 2.0 * math.pi * moment / jnp.array([LX, LY, total_z], f32)[None]
    alpha = jnp.stack([jnp.cos(hop), -jnp.sin(hop)], -1)
    alpha = jnp.concatenate(
        [jnp.broadcast_to(jnp.array([-1.0, 0.0], f32), (nmom, 1, 2)), alpha], 1
    ).reshape(-1)
    local = contraction_list.shape[0]
    element = contraction_list[:, 0]
    per = nmom * NDISP
    t, m, d = element // per, (element // NDISP) % nmom, element % NDISP
    row = jnp.stack([t * NDISP, t * NDISP + d, m, m * NDISP + d], 1).reshape(-1)
    row = jnp.pad(row, (0, 128 - row.shape[0])).reshape(1, 128)
    vmem = pl.BlockSpec(memory_space=pltpu.VMEM)
    smem = pl.BlockSpec(memory_space=pltpu.SMEM)
    tile = (local, 2, nvec, nvec)
    dma = pltpu.SemaphoreType.DMA
    elem = pl.pallas_call(
        functools.partial(
            elemental_kernel,
            (nspace, ndiag, inner, local, slices, nvec, plane, 0.5 * scale),
        ),
        out_shape=jax.ShapeDtypeStruct(tile, bf16),
        in_specs=[vmem, smem, vmem, vmem, vmem, vmem],
        out_specs=vmem,
        scratch_shapes=[
            pltpu.VMEM((slices, 2, 3, nvec, plane), bf16),
            pltpu.VMEM((slices * NDISP, 2 * nvec, 3 * plane), bf16),
            pltpu.VMEM((ndev, 1, 128), jnp.int32),
            pltpu.SMEM((ndev, 1, 128), jnp.int32),
            pltpu.VMEM((nspace,) + tile, bf16),
            pltpu.VMEM((nspace,) + tile, bf16),
            pltpu.VMEM((outer,) + tile, bf16),
            pltpu.VMEM((outer,) + tile, bf16),
            pltpu.VMEM((outer,) + tile, bf16),
            pltpu.VMEM((outer,) + tile, bf16),
            pltpu.VMEM(tile, f32),
            dma((slices,)), dma((slices,)),
            dma((ndev,)), dma((ndev,)), dma,
            dma((nspace,)), dma((nspace,)),
            dma((outer,)), dma((outer,)),
            dma((outer,)), dma((outer,)),
        ],
        compiler_params=pltpu.CompilerParams(
            collective_id=0, has_side_effects=True, vmem_limit_bytes=48 * 1024 * 1024
        ),
    )(
        row, alpha, cosine, sine, gauge_links.reshape(slices, 3, 2, 3, 3, plane),
        eigvecs.reshape(slices, 2, 3, nvec, plane),
    )
    count, spins = perambulators.shape[:2]
    width = perambulators.shape[4]
    tau = perambulators.reshape(count, spins, 2 * nvec, width)
    pick = jnp.stack([contraction_list[:, 2] - position * count, contraction_list[:, 1]], 1)
    out = pl.pallas_call(
        diagram_kernel,
        grid_spec=pltpu.PrefetchScalarGridSpec(
            num_scalar_prefetch=2,
            grid=(local,),
            in_specs=[
                pl.BlockSpec((1, 2, nvec, nvec), lambda i, pick, spin: (i, 0, 0, 0)),
                pl.BlockSpec((1, spins, 2 * nvec, width), lambda i, pick, spin: (pick[i, 0], 0, 0, 0)),
            ],
            out_specs=pl.BlockSpec((1, spins, 2 * nvec, width), lambda i, pick, spin: (i, 0, 0, 0)),
        ),
        out_shape=jax.ShapeDtypeStruct((local, spins, 2 * nvec, width), bf16),
    )(pick, spin_mix.reshape(spin_mix.shape[0], -1), elem, tau)
    return out.reshape(local, spins, 2, nvec, width)


def solution(mesh):
    placed = (
        P("cfg", None, None, None, ("space", "diag"), None),
        P("cfg", None, None, None, None, ("space", "diag"), None),
        P(),
        P(),
        P(("cfg", "space", "diag"), None, None, None, None),
        P(("space", "diag"), None),
    )
    return jax.shard_map(
        body,
        mesh=mesh,
        in_specs=placed,
        out_specs=P(("cfg", "space", "diag"), None, None, None, None),
        check_vma=False,
    )
```

profile of v0, /device:TPU:13, one launch (start us, length us, event | category | flops | bytes accessed | tf_op | source)
XLA Modules:
  0.0 63.1 jit_solution(8134937505576724100)
XLA Ops:
  0.0 0.7 %convert_element_type.20 = f32[4,3]{1,0:T(4,128)S(1)} convert(s32[4,3]{1,0:T(4,128)} %param.10) | non-fusion elementwise | flops 12 | bytes 96 | tf_op jit(solution)/shard_map/convert_element_type | solution.py:261
  0.7 0.2 slice_reduce_fusion.1
  0.9 0.7 %fusion.7 = (s32[2,1]{1,0:T(2,128)S(1)}, s32[2,1]{1,0:T(2,128)S(1)}, pred[2,1]{1,0:T(4,128)(4,1)S(1)}) fusion(s32[2,3]{1,0:T(2,128)} %param.13), kind=kLoop, calls=%fused_computation.39 | loop fusion | flops 50 | bytes 26 | tf_op jit(solution)/shard_map/add | solution.py:277
  1.6 0.9 %multiply_add_fusion = (s32[2,1]{1,0:T(2,128)S(1)}, s32[2,1]{1,0:T(2,128)S(1)}, s32[2,1]{1,0:T(2,128)S(1)}, s32[2,1]{1,0:T(2,128)S(1)}) fusion(pred[2,1]{1,0:T(4,128)(4,1)S(1)} %get-tuple-element.10, s32[2,3]{1,0:T(2,128)} %param.13, s32[]{:T(128)S(6)} %mul.62), kind=kLoop, calls=%fused_computation.32 | loop fusion | flops 64 | bytes 62 | tf_op jit(solution)/shard_map/add | solution.py:277
  2.4 0.1 pad_add_fusion.1
  2.5 0.1 reshape.50
  2.6 0.7 %pad_add_fusion.pick_ref = s32[2,2]{1,0:T(2,128)} fusion(s32[2,1]{1,0:T(2,128)S(1)} %get-tuple-element.18, s32[2,1]{1,0:T(2,128)S(1)} %get-tuple-element.17), kind=kLoop, calls=%fused_computation.28 | loop fusion | flops 4 | bytes 32 | tf_op jit(solution)/shard_map/stack | solution.py:319
  3.3 0.7 %cosine_bitcast_fusion = (f32[4,3,1]{1,0,2:T(4,128)S(1)}, f32[4,3,1]{1,0,2:T(4,128)S(1)}) fusion(s32[4,3]{1,0:T(4,128)} %param.10), kind=kLoop, calls=%fused_computation.11 | loop fusion | flops 36 | bytes 144 | tf_op jit(solution)/shard_map/stack | solution.py:269
  4.0 0.7 %broadcast_in_dim.2 = f32[4,1,2]{1,0,2:T(4,128)S(1)} broadcast(f32[2]{0:T(128)} %constant.92.clone), dimensions={2} | broadcast | bytes 40 | tf_op jit(solution)/shard_map/broadcast_in_dim | solution.py:271
  4.7 0.1 maximum_maximum_fusion
  4.8 0.1 copy.11
  4.9 0.1 reshape.52.alpha_ref
  5.0 0.1 fusion
  5.1 1.4 %copy.14.spin_ref = f32[16,16]{1,0:T(8,128)} copy(f32[16,16]{0,1:T(8,128)} %bitcast.17) | data formatting | bytes 2048 | tf_op jit(solution)/shard_map/reshape | solution.py:332
  6.5 1.0 %copy.17 = f32[4,3,2,3,3,1,256]{6,4,3,2,1,0,5:T(4,128)S(1)} copy(f32[4,3,2,3,3,1,256]{6,5,4,3,2,1,0:T(1,128)} %param.9) | data formatting | bytes 442368 | tf_op jit(solution)/shard_map/reshape | solution.py:313
  7.5 0.0 copy-start
  7.5 1.4 %copy-done = bf16[4,2,3,128,1,256]{5,3,4,2,1,0:T(8,128)(2,1)S(1)} copy-done((bf16[4,2,3,128,1,256]{5,3,4,2,1,0:T(8,128)(2,1)S(1)}, bf16[4,2,3,128,1,256]{5,3,4,2,1,0:T(8,128)(2,1)}, u32[]{:S(2)}) %copy-start) | copy-done | bytes 1572888
  8.9 49.0 %shard_map.82.elem_ref = bf16[2,2,128,128]{3,2,1,0:T(8,128)(2,1)S(1)} custom-call(s32[1,128]{1,0:T(1,128)S(1)} %pad_bitcast_fusion.list_ref, f32[32]{0:T(128)S(1)} %reshape.52.alpha_ref, f32[4,256]{1,0:T(4,128)S(1)} %get-tuple-element.14.cos_ref, f32[4,256]{1,0:T(4,128)S(1)} %get-tuple-element.13.sin_ref, f32[4,3,2,3,3,256]{5,4,3,2,1,0:T(4,128)S(1)} %bitcast.15, ...), custom_call_target="tpu_custom_call" | custom-call | tf_op jit(solution)/shard_map/pallas_call | solution.py:283
  57.9 0.0 copy-start.1
  57.9 0.6 copy-done.1
  58.5 4.5 %shard_map.83 = bf16[2,4,256,512]{3,2,1,0:T(8,128)(2,1)} custom-call(s32[2,2]{1,0:T(2,128)} %pad_add_fusion.pick_ref, f32[16,16]{1,0:T(8,128)} %copy.14.spin_ref, bf16[2,2,128,128]{3,2,1,0:T(8,128)(2,1)} %copy-done.1, bf16[2,4,256,512]{3,2,1,0:T(8,128)(2,1)} %bitcast.16), custom_call_target="tpu_custom_call" | custom-call | tf_op jit(solution)/shard_map/pallas_call | solution.py:320
  (2 shorter events, 0.0 us)
Async XLA Ops:
  7.5 1.4 %copy-start = (bf16[4,2,3,128,1,256]{5,3,4,2,1,0:T(8,128)(2,1)S(1)}, bf16[4,2,3,128,1,256]{5,3,4,2,1,0:T(8,128)(2,1)}, u32[]{:S(2)}) copy-start(bf16[4,2,3,128,1,256]{5,3,4,2,1,0:T(8,128)(2,1)} %param.8) | copy-start | bytes 4718596
  57.9 0.6 %copy-start.1 = (bf16[2,2,128,128]{3,2,1,0:T(8,128)(2,1)}, bf16[2,2,128,128]{3,2,1,0:T(8,128)(2,1)S(1)}, u32[]{:S(2)}) copy-start(bf16[2,2,128,128]{3,2,1,0:T(8,128)(2,1)S(1)} %shard_map.82.elem_ref) | copy-start | bytes 393220
where the time goes:
time: 63.5 us; the launch traced here: 63.1 us
  Pallas kernels  53.5 us (84%)
  local copies, waits for them, and re-layouts  5.44 us (9%)
  other arithmetic  4.08 us (6%)
    pallas_call x1, Pallas kernels, body(): pl.pallas_call(functools.partial(elemental_kernel, (nspace, ndiag, inner,...  49 us
    pallas_call x1, Pallas kernels, body(): pl.pallas_call(diagram_kernel, grid_spec=pltpu.PrefetchScalarGridSpec(num...  4.55 us
    unnamed x4, local copies, waits for them, and re-layouts  2.03 us
    add x2, other arithmetic, body(): row = jnp.stack([t * NDISP, t * NDISP + d, m, m * NDISP + d], 1).reshape(-1)  1.55 us
    reshape x1, local copies, waits for them, and re-layouts, body(): spin_mix.reshape(spin_mix.shape[0], -1)  1.36 us

commit v1 on v0

v1 whole, which is shorter than its diff:
```python
import functools
import math

import jax
import jax.numpy as jnp
from jax import lax
from jax.experimental import pallas as pl
from jax.experimental.pallas import tpu as pltpu
from jax.sharding import PartitionSpec as P

LX = 16
LY = 16
NDISP = 4
CHUNK = 16
MESH = pl.DeviceIdType.MESH
NT = (((1,), (1,)), ((), ()))
f32 = jnp.float32
bf16 = jnp.bfloat16


def elemental_kernel(
    dims, list_ref, mom_ref, link_ref, eig_hbm, out_ref,
    eig_ref, cos_ref, sin_ref, ar_ref, ai_ref, above, fields, lists, table, part1, recv1, part2, recv2, part3, recv3, own,
    e_local, v_send, v_recv, l_send, l_recv, l_local, s1, r1, s2, r2, s3, r3,
):
    nspace, ndiag, inner, local, slices, nvec, plane, factor = dims
    ndev = nspace * ndiag
    outer = nspace // inner
    space = lax.axis_index("space")
    core = lax.axis_index("diag")
    cfg = lax.axis_index("cfg")
    me = space * ndiag + core
    zpos = space // inner
    ypos = lax.rem(space, inner)

    def device(index):
        return (cfg, index // ndiag, lax.rem(index, ndiag))

    def e_copy(t):
        return pltpu.make_async_copy(eig_hbm.at[t], eig_ref.at[t], e_local.at[t])

    for t in range(slices):
        e_copy(t).start()

    barrier = pltpu.get_barrier_semaphore()

    @pl.loop(1, ndev)
    def _(k):
        pl.semaphore_signal(
            barrier, inc=1, device_id=device(lax.rem(me + k, ndev)), device_id_type=MESH
        )

    column = lax.broadcasted_iota(jnp.int32, (1, 128), 1)
    packed = jnp.zeros((1, 128), jnp.int32)
    for i in range(local):
        packed = jnp.where(column == i, list_ref[i, 0], packed)
    lists[0] = packed

    nmom = mom_ref.shape[0]
    flat = lax.broadcasted_iota(jnp.int32, (1, plane), 1)
    xcoord = lax.rem(flat, LX).astype(f32)
    ycoord = lax.div(flat, LX).astype(f32)
    zcoord = lax.convert_element_type(me, f32)
    rows, hops = [], []
    for m in range(nmom):
        mom = [mom_ref[m, axis].astype(f32) for axis in range(3)]
        rows.append(
            2.0 * math.pi * (mom[0] * xcoord / LX + mom[1] * ycoord / LY + mom[2] * zcoord / ndev)
        )
        hops.append(jnp.full((1, nvec), math.pi, f32))
        for axis, size in enumerate((LX, LY, ndev)):
            hops.append(jnp.full((1, nvec), mom[axis] * (2.0 * math.pi / size), f32))
    angle = jnp.concatenate(rows, 0)
    cos_ref[...] = jnp.cos(angle)
    sin_ref[...] = jnp.sin(angle)
    hop = jnp.concatenate(hops, 0)
    plain = lax.rem(lax.broadcasted_iota(jnp.int32, hop.shape, 0), NDISP) == 0
    ar_ref[...] = jnp.where(plain, -1.0, jnp.cos(hop))
    ai_ref[...] = jnp.where(plain, 0.0, -jnp.sin(hop))

    pl.semaphore_wait(barrier, ndev - 1)

    def v_copy(t):
        return pltpu.make_async_remote_copy(
            src_ref=eig_hbm.at[t], dst_ref=above.at[t],
            send_sem=v_send.at[t], recv_sem=v_recv.at[t],
            device_id=device(lax.rem(me + ndev - 1, ndev)), device_id_type=MESH,
        )

    def l_copy(k):
        return pltpu.make_async_remote_copy(
            src_ref=lists.at[0], dst_ref=lists.at[k],
            send_sem=l_send.at[k], recv_sem=l_recv.at[k],
            device_id=device(lax.rem(me + k, ndev)), device_id_type=MESH,
        )

    for t in range(slices):
        v_copy(t).start()

    @pl.loop(1, ndev)
    def _(k):
        l_copy(k).start()

    lane = lax.broadcasted_iota(jnp.int32, (CHUNK, plane), 1)
    edge = lax.rem(lane, LX) == LX - 1

    def displace(t, direction, source):
        @pl.loop(0, nvec // CHUNK)
        def _(i):
            rows = pl.multiple_of(i * CHUNK, CHUNK)
            vec = []
            for p in range(2):
                line = []
                for c in range(3):
                    v = source[t, p, c, pl.ds(rows, CHUNK), :].astype(f32)
                    if direction == 0:
                        v = jnp.where(
                            edge, pltpu.roll(v, LX - 1, 1), pltpu.roll(v, plane - 1, 1)
                        )
                    elif direction == 1:
                        v = pltpu.roll(v, plane - LX, 1)
                    line.append(v)
                vec.append(line)
            for row in range(3):
                real = imag = None
                for col in range(3):
                    mr = link_ref[t, direction, 0, row, col]
                    mi = link_ref[t, direction, 1, row, col]
                    re = mr * vec[0][col] - mi * vec[1][col]
                    im = mr * vec[1][col] + mi * vec[0][col]
                    real = re if real is None else real + re
                    imag = im if imag is None else imag + im
                lanes = slice(row * plane, (row + 1) * plane)
                fields[t * NDISP + direction + 1, pl.ds(rows, CHUNK), lanes] = real.astype(bf16)
                fields[
                    t * NDISP + direction + 1, pl.ds(nvec + rows, CHUNK), lanes
                ] = imag.astype(bf16)

    @pl.loop(0, slices)
    def _(t):
        e_copy(t).wait()
        for p in range(2):
            for c in range(3):
                fields[
                    t * NDISP, p * nvec:(p + 1) * nvec, c * plane:(c + 1) * plane
                ] = eig_ref[t, p, c]
        displace(t, 0, eig_ref)
        displace(t, 1, eig_ref)

    @pl.loop(1, ndev)
    def _(k):
        l_copy(k).wait()

    to_smem = pltpu.make_async_copy(lists, table, l_local)
    to_smem.start()
    to_smem.wait()

    @pl.loop(0, slices)
    def _(t):
        v_copy(t).wait()
        displace(t, 2, above)

    def item(dest, i):
        slot = lax.rem(me + ndev - dest, ndev)
        entry = table[slot, 0, i]
        time = lax.div(entry, nmom * NDISP)
        m = lax.rem(lax.div(entry, NDISP), nmom)
        d = lax.rem(entry, NDISP)
        ar = ar_ref[pl.ds(m * NDISP + d, 1), :]
        ai = ai_ref[pl.ds(m * NDISP + d, 1), :]
        cosine = cos_ref[pl.ds(m, 1), :]
        sine = sin_ref[pl.ds(m, 1), :]
        cosine = jnp.concatenate([cosine] * 3, 1)
        sine = jnp.concatenate([sine] * 3, 1)
        v = fields[time * NDISP]
        x = fields[time * NDISP + d].astype(f32)
        xr, xi = x[:nvec], x[nvec:]
        a, b = cosine * xr, sine * xi
        g, h = cosine * xi, sine * xr
        y = jnp.concatenate([(a + b).astype(bf16), (g - h).astype(bf16)], 0)
        z = jnp.concatenate([(a - b).astype(bf16), (g + h).astype(bf16)], 0)
        first = lax.dot_general(v, y, NT, preferred_element_type=f32)
        second = lax.dot_general(z, v, NT, preferred_element_type=f32)
        g1r = first[:nvec, :nvec] + first[nvec:, nvec:]
        g1i = first[:nvec, nvec:] - first[nvec:, :nvec]
        g2r = second[:nvec, :nvec] + second[nvec:, nvec:]
        g2i = second[:nvec, nvec:] - second[nvec:, :nvec]
        return (
            (g1r - (ar * g2r - ai * g2i)) * factor,
            (g1i - (ar * g2i + ai * g2r)) * factor,
        )

    def copy1(j):
        return pltpu.make_async_remote_copy(
            src_ref=part1.at[j], dst_ref=recv1.at[j], send_sem=s1.at[j], recv_sem=r1.at[j],
            device_id=(cfg, space, 1 - core), device_id_type=MESH,
        )

    def copy2(j):
        return pltpu.make_async_remote_copy(
            src_ref=part2.at[j], dst_ref=recv2.at[j], send_sem=s2.at[j], recv_sem=r2.at[j],
            device_id=(cfg, zpos * inner + (1 - ypos), core), device_id_type=MESH,
        )

    def copy3(j):
        return pltpu.make_async_remote_copy(
            src_ref=part3.at[j], dst_ref=recv3.at[j], send_sem=s3.at[j], recv_sem=r3.at[j],
            device_id=(cfg, lax.rem(zpos + 1 + j, outer) * inner + ypos, core),
            device_id_type=MESH,
        )

    def target(j):
        zway = lax.rem(zpos + 1 + lax.rem(j, outer), outer)
        yway = lax.rem(1 - ypos + j // outer, inner)
        return (zway * inner + yway) * ndiag

    def send_partner(j):
        for i in range(local):
            real, imag = item(target(j) + (1 - core), i)
            part1[j, i, 0] = real.astype(bf16)
            part1[j, i, 1] = imag.astype(bf16)
        copy1(j).start()

    def chip_sum(j):
        for i in range(local):
            real, imag = item(target(j) + core, i)
            own[j, i, 0] = real
            own[j, i, 1] = imag
        copy1(j).wait()

    send_partner(0)

    @pl.loop(0, outer)
    def _(j):
        send_partner(j + 1)
        chip_sum(j)
        part2[j] = (own[j] + recv1[j].astype(f32)).astype(bf16)
        copy2(j).start()

    @pl.loop(0, outer - 1)
    def _(j):
        k = j + outer
        send_partner(k + 1)
        chip_sum(k)
        copy2(j).wait()
        part3[j] = (own[k] + recv1[k].astype(f32) + recv2[j].astype(f32)).astype(bf16)
        copy3(j).start()

    last = nspace - 1
    chip_sum(last)
    copy2(outer - 1).wait()
    own[last] = own[last] + recv1[last].astype(f32) + recv2[outer - 1].astype(f32)

    @pl.loop(0, outer - 1)
    def _(j):
        copy3(j).wait()
        own[last] = own[last] + recv3[j].astype(f32)

    out_ref[...] = own[last].astype(bf16)


def diagram_kernel(pick_ref, spin_ref, elem_ref, tau_ref, out_ref):
    d = pl.program_id(0)
    g = pick_ref[d, 1]
    spins = tau_ref.shape[1]
    er, ei = elem_ref[0, 0], elem_ref[0, 1]
    square = jnp.concatenate(
        [jnp.concatenate([er, -ei], 1), jnp.concatenate([ei, er], 1)], 0
    )
    width = tau_ref.shape[3]
    step = 256 if width % 256 == 0 else width
    for start in range(0, width, step):
        blocks = [
            jnp.dot(square, tau_ref[0, s, :, start:start + step], preferred_element_type=f32)
            for s in range(spins)
        ]
        for r in range(spins):
            mixed = spin_ref[r, 0, g] * blocks[0]
            for s in range(1, spins):
                mixed = mixed + spin_ref[r, s, g] * blocks[s]
            out_ref[0, r, :, start:start + step] = mixed.astype(bf16)


def body(eigvecs, gauge_links, momenta, spin_mix, perambulators, contraction_list):
    slices, _, colors, nvec, depth, plane = eigvecs.shape
    assert depth == 1 and colors == 3
    nspace, ndiag = lax.axis_size("space"), lax.axis_size("diag")
    assert ndiag == 2 and nspace % 2 == 0
    inner = 2
    outer = nspace // inner
    ndev = nspace * ndiag
    scale = 1.0 / math.sqrt(3 * plane * ndev)
    nmom = momenta.shape[0]
    local = contraction_list.shape[0]
    vmem = pl.BlockSpec(memory_space=pltpu.VMEM)
    smem = pl.BlockSpec(memory_space=pltpu.SMEM)
    tile = (local, 2, nvec, nvec)
    dma = pltpu.SemaphoreType.DMA
    elem = pl.pallas_call(
        functools.partial(
            elemental_kernel,
            (nspace, ndiag, inner, local, slices, nvec, plane, 0.5 * scale),
        ),
        out_shape=jax.ShapeDtypeStruct(tile, bf16),
        in_specs=[smem, smem, vmem, pl.BlockSpec(memory_space=pltpu.HBM)],
        out_specs=vmem,
        scratch_shapes=[
            pltpu.VMEM((slices, 2, 3, nvec, plane), bf16),
            pltpu.VMEM((nmom, plane), f32),
            pltpu.VMEM((nmom, plane), f32),
            pltpu.VMEM((nmom * NDISP, nvec), f32),
            pltpu.VMEM((nmom * NDISP, nvec), f32),
            pltpu.VMEM((slices, 2, 3, nvec, plane), bf16),
            pltpu.VMEM((slices * NDISP, 2 * nvec, 3 * plane), bf16),
            pltpu.VMEM((ndev, 1, 128), jnp.int32),
            pltpu.SMEM((ndev, 1, 128), jnp.int32),
            pltpu.VMEM((nspace,) + tile, bf16),
            pltpu.VMEM((nspace,) + tile, bf16),
            pltpu.VMEM((outer,) + tile, bf16),
            pltpu.VMEM((outer,) + tile, bf16),
            pltpu.VMEM((outer,) + tile, bf16),
            pltpu.VMEM((outer,) + tile, bf16),
            pltpu.VMEM((nspace,) + tile, f32),
            dma((slices,)), dma((slices,)), dma((slices,)),
            dma((ndev,)), dma((ndev,)), dma,
            dma((nspace,)), dma((nspace,)),
            dma((outer,)), dma((outer,)),
            dma((outer,)), dma((outer,)),
        ],
        compiler_params=pltpu.CompilerParams(
            collective_id=0, has_side_effects=True, vmem_limit_bytes=63 * 1024 * 1024
        ),
    )(
        contraction_list, momenta, gauge_links,
        eigvecs.reshape(slices, 2, 3, nvec, plane),
    )
    count, spins = perambulators.shape[:2]
    halves = 2
    width = perambulators.shape[4]
    tau = perambulators.reshape(count, spins, 2 * nvec, width)
    out = pl.pallas_call(
        diagram_kernel,
        grid_spec=pltpu.PrefetchScalarGridSpec(
            num_scalar_prefetch=2,
            grid=(local, halves),
            in_specs=[
                pl.BlockSpec((1, 2, nvec, nvec), lambda i, h, pick, spin: (i, 0, 0, 0)),
                pl.BlockSpec(
                    (1, spins, 2 * nvec, width // halves),
                    lambda i, h, pick, spin: (lax.rem(pick[i, 2], count), 0, 0, h),
                ),
            ],
            out_specs=pl.BlockSpec(
                (1, spins, 2 * nvec, width // halves), lambda i, h, pick, spin: (i, 0, 0, h)
            ),
        ),
        out_shape=jax.ShapeDtypeStruct((local, spins, 2 * nvec, width), bf16),
    )(contraction_list, spin_mix.transpose(1, 2, 0), elem, tau)
    return out.reshape(local, spins, 2, nvec, width)


def solution(mesh):
    placed = (
        P("cfg", None, None, None, ("space", "diag"), None),
        P("cfg", None, None, None, None, ("space", "diag"), None),
        P(),
        P(),
        P(("cfg", "space", "diag"), None, None, None, None),
        P(("space", "diag"), None),
    )
    return jax.shard_map(
        body,
        mesh=mesh,
        in_specs=placed,
        out_specs=P(("cfg", "space", "diag"), None, None, None, None),
        check_vma=False,
    )
```

time: 63.5 us -> 57.1 us (0.90)
  local copies, waits for them, and re-layouts: 5.44 us -> 0 us
  other arithmetic: 4.08 us -> 0 us
  Pallas kernels: 53.5 us -> 56.8 us
    reshape x5 -> x0, local copies, waits for them, and re-layouts: 2.56 us -> none  [the longest x1 1.36 us: body(): spin_mix.reshape(spin_mix.shape[0], -1)]
    pallas_call x1, Pallas kernels: 49 us -> 51.4 us  [body(): pl.pallas_call(functools.partial(elemental_kernel, (nspace, ndiag, inner,...]
    unnamed x4 -> x0, local copies, waits for them, and re-layouts: 2.03 us -> none
    add x2 -> x0, other arithmetic: 1.55 us -> none  [body(): row = jnp.stack([t * NDISP, t * NDISP + d, m, m * NDISP + d], 1).reshape(-1)]
    another operation x3 -> x0, other arithmetic: 1.45 us -> none  [the longest x1 0.72 us: body(): alpha = jnp.stack([jnp.cos(hop), -jnp.sin(hop)], -1)]
    pallas_call x1, Pallas kernels: 4.55 us -> 5.47 us  [body(): pl.pallas_call(diagram_kernel, grid_spec=pltpu.PrefetchScalarGridSpec(num...]
    broadcast_in_dim x1 -> x0, local copies, waits for them, and re-layouts: 0.73 us -> none  [body(): jnp.broadcast_to(jnp.array([-1.0, 0.0], f32), (nmom, 1, 2))]
    convert_element_type x2 -> x0, other arithmetic: 0.69 us -> none  [the longest x1 0.68 us: body(): moment = momenta.astype(f32)]
where the time goes in v1:
time: 57.1 us; the launch traced here: 56.8 us
  Pallas kernels  56.8 us (99%)
    pallas_call x1, Pallas kernels, body(): pl.pallas_call(functools.partial(elemental_kernel, (nspace, ndiag, inner,...  51.4 us
    pallas_call x1, Pallas kernels, body(): pl.pallas_call(diagram_kernel, grid_spec=pltpu.PrefetchScalarGridSpec(num...  5.47 us

profile of v1, /device:TPU:13, one launch (start us, length us, event | category | flops | bytes accessed | tf_op | source)
XLA Modules:
  0.0 56.8 jit_solution(6417435610057915671)
XLA Ops:
  0.0 51.4 %shard_map.64.elem_ref = bf16[2,2,128,128]{3,2,1,0:T(8,128)(2,1)} custom-call(s32[2,3]{1,0:T(2,128)} %pick_ref.1, s32[4,3]{1,0:T(4,128)} %mom_ref.1, f32[4,3,2,3,3,1,256]{6,5,4,3,2,1,0:T(1,128)} %link_ref.1, bf16[4,2,3,128,256]{4,3,2,1,0:T(8,128)(2,1)} %bitcast.5), custom_call_target="tpu_custom_call" | custom-call | tf_op jit(solution)/shard_map/pallas_call | solution.py:299
  51.4 5.5 %shard_map.65 = bf16[2,4,256,512]{3,2,1,0:T(8,128)(2,1)} custom-call(s32[2,3]{1,0:T(2,128)} %pick_ref.1, f32[4,4,16]{2,1,0:T(4,128)} %bitcast.6, bf16[2,2,128,128]{3,2,1,0:T(8,128)(2,1)} %shard_map.64.elem_ref, bf16[2,4,256,512]{3,2,1,0:T(8,128)(2,1)} %bitcast.4), custom_call_target="tpu_custom_call" | custom-call | tf_op jit(solution)/shard_map/pallas_call | solution.py:341

commit v2 on v1

--- a/solution.py
+++ b/solution.py
@@ -335,7 +335,7 @@
         eigvecs.reshape(slices, 2, 3, nvec, plane),
     )
     count, spins = perambulators.shape[:2]
-    halves = 2
+    halves = 1
     width = perambulators.shape[4]
     tau = perambulators.reshape(count, spins, 2 * nvec, width)
     out = pl.pallas_call(

time: 57.1 us -> 56.2 us (0.984)
  Pallas kernels: 56.8 us -> 55.9 us
    pallas_call x1, Pallas kernels: 5.47 us -> 4.57 us  [body(): pl.pallas_call(diagram_kernel, grid_spec=pltpu.PrefetchScalarGridSpec(num...]
where the time goes in v2:
time: 56.2 us; the launch traced here: 55.9 us
  Pallas kernels  55.9 us (99%)
    pallas_call x1, Pallas kernels, body(): pl.pallas_call(functools.partial(elemental_kernel, (nspace, ndiag, inner,...  51.4 us
    pallas_call x1, Pallas kernels, body(): pl.pallas_call(diagram_kernel, grid_spec=pltpu.PrefetchScalarGridSpec(num...  4.57 us

profile of v2, /device:TPU:13, one launch (start us, length us, event | category | flops | bytes accessed | tf_op | source)
XLA Modules:
  0.0 55.9 jit_solution(17395278347952819178)
XLA Ops:
  0.0 51.4 %shard_map.64.elem_ref = bf16[2,2,128,128]{3,2,1,0:T(8,128)(2,1)} custom-call(s32[2,3]{1,0:T(2,128)} %pick_ref.1, s32[4,3]{1,0:T(4,128)} %mom_ref.1, f32[4,3,2,3,3,1,256]{6,5,4,3,2,1,0:T(1,128)} %link_ref.1, bf16[4,2,3,128,256]{4,3,2,1,0:T(8,128)(2,1)} %bitcast.5), custom_call_target="tpu_custom_call" | custom-call | tf_op jit(solution)/shard_map/pallas_call | solution.py:299
  51.4 4.6 %shard_map.65 = bf16[2,4,256,512]{3,2,1,0:T(8,128)(2,1)} custom-call(s32[2,3]{1,0:T(2,128)} %pick_ref.1, f32[4,4,16]{2,1,0:T(4,128)} %bitcast.6, bf16[2,2,128,128]{3,2,1,0:T(8,128)(2,1)} %shard_map.64.elem_ref, bf16[2,4,256,512]{3,2,1,0:T(8,128)(2,1)} %bitcast.4), custom_call_target="tpu_custom_call" | custom-call | tf_op jit(solution)/shard_map/pallas_call | solution.py:341
